TPU v7x, 32 devices: a whole 2x2x4 slice. The times are simulated.
32 devices in a mesh: dp: 2 (over x), row: 4 (over z), col: 4 (over y, core).
Axes of the slice: x: 2, y: 2, z: 4, core: 2. Of those that a mesh axis runs over, the one named last changes fastest.
Arguments:
- features: bfloat16 [2, 128, 128, 320], P('dp', 'row', 'col'), may hold values from -20 to 20
- norm1_gain: float32 [320], replicated, may hold values from 0.1 to 1.9
- conv1_kernel: bfloat16 [320, 9, 320], P('dp'), may hold values from -0.109375 to 0.109375
- norm2_gain: float32 [320], replicated, may hold values from 0.1 to 1.9
- conv2_kernel: bfloat16 [320, 9, 320], P('dp'), may hold values from -0.109375 to 0.109375
Outputs:
- block_out: bfloat16 [2, 128, 128, 320], P('dp', 'row', 'col')
All inputs are finite; a program needn't handle non-finite values.
Results may differ from a plain program's by a relative error of at most 0.007.
Values may be sent and summed in bfloat16 or wider, within the bound.
No kernel may reach another device: no remote copies, remote signals or barrier semaphores. Data moves between devices by JAX's collectives and lax.ppermute only.
A program may use at most 64 MiB of HBM per device.

v0:
```python
import jax
import jax.numpy as jnp
from jax import lax
from jax.sharding import PartitionSpec as P

GROUPS = 32
EPS = 1e-05


def extended(value, sides, width):
    for axis, dim in sides:
        size, length = (lax.axis_size(axis), value.shape[dim])
        up = [(i, (i + 1) % size) for i in range(size - 1)]
        down = [(j, i) for i, j in up]
        last = lax.slice_in_dim(value, length - width, length, axis=dim)
        initial = lax.slice_in_dim(value, 0, width, axis=dim)
        before = lax.ppermute(last, axis, up)
        after = lax.ppermute(initial, axis, down)
        value = jnp.concatenate([before, value, after], axis=dim)
    return value


def normalize(values, scale_gain, count):
    batch_dev, tile_rows, tile_cols, width = values.shape
    grouped = values.astype(jnp.float32).reshape(
        batch_dev, tile_rows * tile_cols, GROUPS, width // GROUPS
    )
    totals, squares = lax.psum(
        (jnp.sum(grouped, axis=(1, 3)), jnp.sum(grouped * grouped, axis=(1, 3))), ("row", "col")
    )
    average_flat = totals / count
    spread = squares / count - average_flat * average_flat
    centred = grouped - average_flat[:, None, :, None]
    scaled = centred * lax.rsqrt(spread + EPS)[:, None, :, None]
    normed = scaled.reshape(values.shape) * scale_gain
    return jax.nn.silu(normed).astype(jnp.bfloat16)


def tap_stack(values):
    padded = extended(values, (("row", 1), ("col", 2)), 1)
    tile_rows, tile_cols, width = (values.shape[1], values.shape[2], values.shape[3])
    pieces = [
        padded[:, shift_row : shift_row + tile_rows, shift_col : shift_col + tile_cols, :]
        for shift_row in range(3)
        for shift_col in range(3)
    ]
    return jnp.concatenate(pieces, axis=-1).reshape(-1, 9 * width)


def finish(stacked, whole_kernel, skip_flat):
    flat_kernel = whole_kernel.reshape(whole_kernel.shape[0], -1)
    result = lax.dot_general(
        stacked, flat_kernel, (((1,), (1,)), ((), ())), preferred_element_type=jnp.float32
    )
    if skip_flat is not None:
        result = result + skip_flat.astype(jnp.float32)
    return result.astype(jnp.bfloat16)


def convolve_gathered(stacked, kernel, skip_flat):
    whole_kernel = lax.all_gather(kernel, "dp", axis=0, tiled=True)
    return finish(stacked, whole_kernel, skip_flat)


def local(features, norm1_gain, conv1_kernel, norm2_gain, conv2_kernel):
    batch_dev, tile_rows, tile_cols, width = features.shape
    count = tile_rows * tile_cols * lax.axis_size("row") * lax.axis_size("col") * (width // GROUPS)
    first_act = normalize(features, norm1_gain, count)
    first_stack = tap_stack(first_act)
    middle = convolve_gathered(first_stack, conv1_kernel, None)
    middle = middle.reshape(batch_dev, tile_rows, tile_cols, width)
    second_act = normalize(middle, norm2_gain, count)
    second_stack = tap_stack(second_act)
    skip_flat = features.reshape(-1, width)
    block_out = convolve_gathered(second_stack, conv2_kernel, skip_flat)
    return block_out.reshape(batch_dev, tile_rows, tile_cols, width)


def solution(mesh):
    return jax.shard_map(
        local,
        mesh=mesh,
        in_specs=(P("dp", "row", "col", None), P(), P("dp", None, None), P(), P("dp", None, None)),
        out_specs=P("dp", "row", "col", None),
        check_vma=False,
    )
```

profile of v0, /device:TPU:9, one launch (start us, length us, event | category | flops | bytes accessed | tf_op | source)
XLA Modules:
  0.0 162.9 jit_solution(10472760439591955007)
XLA Ops:
  7.3 1.4 convert_reduce_fusion
  9.2 22.4 %all-reduce.1 = (f32[1,32]{1,0:T(1,128)S(1)}, f32[1,32]{1,0:T(1,128)S(1)}) all-reduce(f32[1,32]{1,0:T(1,128)S(1)} %bitcast.63, f32[1,32]{1,0:T(1,128)S(1)} %bitcast.61), channel_id=1, replica_groups=mesh['dp'=2,'row'=4,'col'=4] {'row','col'}, use_global_device_ids=true, to_apply=%region_5.6 | all-reduce | flops 64 | bytes 512 | tf_op jit(solution)/shard_map/psum | solution.py:28
  32.0 1.2 multiply_convert_fusion.1
  33.2 3.2 %collective-permute-start = (bf16[1,1,32,320]{3,2,1,0:T(8,128)(2,1)S(1)}, bf16[1,1,32,320]{3,2,1,0:T(8,128)(2,1)S(1)}, u32[]{:S(2)}, u32[]{:S(2)}) collective-permute-start(bf16[1,1,32,320]{3,2,1,0:T(8,128)(2,1)S(1)} %get-tuple-element.39), channel_id=1, source_target_pairs={{0,4},{4,8},{8,12},{1,5},{5,9},{9,13},{2,6},{6,10},{10,14},{3,7},{... | collective-permute-start | bytes 61448 | tf_op jit(solution)/shard_map/ppermute | solution.py:17
  36.4 7.5 %collective-permute-start.1 = (bf16[1,1,32,320]{3,2,1,0:T(8,128)(2,1)S(1)}, bf16[1,1,32,320]{3,2,1,0:T(8,128)(2,1)S(1)}, u32[]{:S(2)}, u32[]{:S(2)}) collective-permute-start(bf16[1,1,32,320]{3,2,1,0:T(8,128)(2,1)S(1)} %get-tuple-element.40), channel_id=1, source_target_pairs={{4,0},{8,4},{12,8},{5,1},{9,5},{13,9},{6,2},{10,6},{14,10},{7,3},{... | collective-permute-start | bytes 61448 | tf_op jit(solution)/shard_map/ppermute | solution.py:18
  44.9 4.8 %collective-permute-start.2 = (bf16[1,34,1,320]{3,2,1,0:T(2,128)(2,1)S(1)}, bf16[1,34,1,320]{3,2,1,0:T(2,128)(2,1)S(1)}, u32[]{:S(2)}, u32[]{:S(2)}) collective-permute-start(bf16[1,34,1,320]{3,2,1,0:T(2,128)(2,1)S(1)} %get-tuple-element.32), channel_id=1, source_target_pairs={{0,1},{1,2},{2,3},{4,5},{5,6},{6,7},{8,9},{9,10},{10,11},{12,13},{... | collective-permute-start | bytes 65288 | tf_op jit(solution)/shard_map/ppermute | solution.py:17
  49.7 3.6 %collective-permute-start.3 = (bf16[1,34,1,320]{3,2,1,0:T(2,128)(2,1)S(1)}, bf16[1,34,1,320]{3,2,1,0:T(2,128)(2,1)S(1)}, u32[]{:S(2)}, u32[]{:S(2)}) collective-permute-start(bf16[1,34,1,320]{3,2,1,0:T(2,128)(2,1)S(1)} %get-tuple-element.31), channel_id=1, source_target_pairs={{1,0},{2,1},{3,2},{5,4},{6,5},{7,6},{9,8},{10,9},{11,10},{13,12},{... | collective-permute-start | bytes 65288 | tf_op jit(solution)/shard_map/ppermute | solution.py:18
  53.4 1.4 pad_maximum_fusion.4
  55.8 1.9 %fusion.6 = (bf16[1,32,32,320]{3,2,1,0:T(8,128)(2,1)S(1)}, bf16[1,32,32,320]{3,2,1,0:T(8,128)(2,1)S(1)}, bf16[1,32,32,320]{3,2,1,0:T(8,128)(2,1)}, bf16[1,32,32,...) fusion(bf16[1,34,33,320]{3,2,1,0:T(8,128)(2,1)S(1)} %get-tuple-element.29, ...), kind=kLoop, calls=%fused_computation.40 | loop fusion | bytes 7864320 | tf_op jit(solution)/shard_map/slice | solution.py:43
  57.7 10.1 %concatenate.96 = bf16[1024,2880]{1,0:T(8,128)(2,1)} concatenate(bf16[1024,320]{1,0:T(8,128)(2,1)} %bitcast.45, bf16[1024,320]{1,0:T(8,128)(2,1)} %bitcast.50, bf16[1024,320]{1,0:T(8,128)(2,1)} %bitcast.44, bf16[1024,320]{1,0:T(8,128)(2,1)} %bitcast.46, bf16[1024,320]{1,0:T(8,128)(2,1)S(1)} %bitcast.39, bf16[1024,320]{1,0:T(8,128)(2,1)S(1)} %bitcast.43, ...), dimensions={1} | concatenate | bytes 11796480 | tf_op jit(solution)/shard_map/concatenate | solution.py:47
  67.8 4.2 %copy.17 = bf16[320,9,320]{0,2,1:T(8,128)(2,1)} copy(bf16[320,9,320]{2,0,1:T(8,128)(2,1)} %all-gather.3.cloned.1.call-done) | data formatting | bytes 3686400 | tf_op jit(solution)/shard_map/all_gather | solution.py:61
  72.0 6.7 %fusion.3 = (f32[320]{0:T(512)S(1)}, f32[320]{0:T(512)S(1)}, f32[1024,320]{0,1:T(8,128)}) fusion(bf16[1024,2880]{1,0:T(8,128)(2,1)} %concatenate.96, bf16[320,2880]{0,1:T(8,128)(2,1)} %bitcast.59), kind=kOutput, calls=%fused_computation.37 | convolution fusion | flops 1889074688 | bytes 9054720 | tf_op jit(solution)/shard_map/dot_general | solution.py:52
  79.2 22.1 %all-reduce = (f32[1,32]{1,0:T(1,128)S(1)}, f32[1,32]{1,0:T(1,128)S(1)}) all-reduce(f32[1,32]{1,0:T(1,128)S(1)} %bitcast.62, f32[1,32]{1,0:T(1,128)S(1)} %bitcast.60), channel_id=1, replica_groups=mesh['dp'=2,'row'=4,'col'=4] {'row','col'}, use_global_device_ids=true, to_apply=%region_11.12 | all-reduce | flops 64 | bytes 512 | tf_op jit(solution)/shard_map/psum | solution.py:28
  101.7 1.8 %copy.18 = f32[1024,320]{1,0:T(8,128)S(1)} copy(f32[1024,320]{0,1:T(8,128)} %get-tuple-element.45) | data formatting | bytes 2621440 | tf_op jit(solution)/shard_map/convert_element_type | solution.py:25
  104.0 1.9 %collective-permute-start.4 = (bf16[1,1,32,320]{3,2,1,0:T(8,128)(2,1)S(1)}, bf16[1,1,32,320]{3,2,1,0:T(8,128)(2,1)S(1)}, u32[]{:S(2)}, u32[]{:S(2)}) collective-permute-start(bf16[1,1,32,320]{3,2,1,0:T(8,128)(2,1)S(1)} %get-tuple-element.35), channel_id=1, source_target_pairs={{0,4},{4,8},{8,12},{1,5},{5,9},{9,13},{2,6},{6,10},{10,14},{3,7},{... | collective-permute-start | bytes 61448 | tf_op jit(solution)/shard_map/ppermute | solution.py:17
  105.9 9.5 %collective-permute-start.5 = (bf16[1,1,32,320]{3,2,1,0:T(8,128)(2,1)S(1)}, bf16[1,1,32,320]{3,2,1,0:T(8,128)(2,1)S(1)}, u32[]{:S(2)}, u32[]{:S(2)}) collective-permute-start(bf16[1,1,32,320]{3,2,1,0:T(8,128)(2,1)S(1)} %get-tuple-element.36), channel_id=1, source_target_pairs={{4,0},{8,4},{12,8},{5,1},{9,5},{13,9},{6,2},{10,6},{14,10},{7,3},{... | collective-permute-start | bytes 61448 | tf_op jit(solution)/shard_map/ppermute | solution.py:18
  115.4 1.4 copy.28
  116.7 4.2 %copy.27 = bf16[320,9,320]{0,2,1:T(8,128)(2,1)} copy(bf16[320,9,320]{2,0,1:T(8,128)(2,1)} %all-gather.5.cloned.1.call-done) | data formatting | bytes 3686400 | tf_op jit(solution)/shard_map/all_gather | solution.py:61
  121.1 1.9 %collective-permute-start.6 = (bf16[1,34,1,320]{3,2,1,0:T(2,128)(2,1)S(1)}, bf16[1,34,1,320]{3,2,1,0:T(2,128)(2,1)S(1)}, u32[]{:S(2)}, u32[]{:S(2)}) collective-permute-start(bf16[1,34,1,320]{3,2,1,0:T(2,128)(2,1)S(1)} %get-tuple-element.28), channel_id=1, source_target_pairs={{0,1},{1,2},{2,3},{4,5},{5,6},{6,7},{8,9},{9,10},{10,11},{12,13},{... | collective-permute-start | bytes 65288 | tf_op jit(solution)/shard_map/ppermute | solution.py:17
  123.0 3.1 %collective-permute-start.7 = (bf16[1,34,1,320]{3,2,1,0:T(2,128)(2,1)S(1)}, bf16[1,34,1,320]{3,2,1,0:T(2,128)(2,1)S(1)}, u32[]{:S(2)}, u32[]{:S(2)}) collective-permute-start(bf16[1,34,1,320]{3,2,1,0:T(2,128)(2,1)S(1)} %get-tuple-element.27), channel_id=1, source_target_pairs={{1,0},{2,1},{3,2},{5,4},{6,5},{7,6},{9,8},{10,9},{11,10},{13,12},{... | collective-permute-start | bytes 65288 | tf_op jit(solution)/shard_map/ppermute | solution.py:18
  127.4 1.1 copy.25
  130.5 2.0 %constant_dynamic-update-slice_fusion.7 = bf16[1024,2880]{0,1:T(8,128)(2,1)} fusion(bf16[1024,320]{0,1:T(8,128)(2,1)} %copy.19), kind=kLoop, calls=%fused_computation.32 | loop fusion | bytes 1310720
  132.5 1.5 fusion.4
  134.0 1.1 copy.21
  135.2 1.1 copy.22
  137.2 2.0 %constant_dynamic-update-slice_fusion.5 = bf16[1024,2880]{0,1:T(8,128)(2,1)} fusion(bf16[1024,2880]{0,1:T(8,128)(2,1)} %constant_dynamic-update-slice_fusion.6, bf16[1024,320]{0,1:T(8,128)(2,1)} %copy.21), kind=kLoop, calls=%fused_computation.30 | loop fusion | bytes 1310720
  140.1 1.4 fusion.2
  141.5 2.2 %copy.23 = bf16[1024,320]{0,1:T(8,128)(2,1)} copy(bf16[1024,320]{1,0:T(8,128)(2,1)} %bitcast.52) | data formatting | bytes 1310720 | tf_op jit(solution)/shard_map/concatenate | solution.py:47
  143.7 1.2 copy.24
  145.2 2.1 %constant_dynamic-update-slice_fusion.3 = bf16[1024,2880]{0,1:T(8,128)(2,1)} fusion(bf16[1024,2880]{0,1:T(8,128)(2,1)} %fusion.2, bf16[1024,320]{0,1:T(8,128)(2,1)} %copy.23), kind=kLoop, calls=%fused_computation.28 | loop fusion | bytes 1310720
  150.0 4.9 %fusion = bf16[1024,320]{0,1:T(8,128)(2,1)S(1)} fusion(f32[1024,320]{0,1:T(8,128)S(1)} %copy-done.8, bf16[1024,2880]{0,1:T(8,128)(2,1)} %constant_dynamic-update-slice_fusion, bf16[320,2880]{0,1:T(8,128)(2,1)S(1)} %bitcast.58), kind=kOutput, calls=%fused_computation.4 | convolution fusion | flops 1888092160 | bytes 9707520 | tf_op jit(solution)/shard_map/dot_general | solution.py:52
  154.9 1.2 copy.29
  (69 shorter events, 13.0 us)
Async XLA Ops:
  6.5 25.4 %copy-start = (bf16[1,32,32,320]{3,2,1,0:T(8,128)(2,1)S(1)}, bf16[1,32,32,320]{3,2,1,0:T(8,128)(2,1)}, u32[]{:S(2)}) copy-start(bf16[1,32,32,320]{3,2,1,0:T(8,128)(2,1)} %param.5) | copy-start | bytes 1966084
  6.5 61.3 %all-gather.3.cloned.1.call-start = ((), (), s32[]{:S(2)}) async-start(), calls=%async_computation | async-start | bytes 3317760 | tf_op jit(solution)/shard_map/all_gather | solution.py:61
  7.3 109.5 %all-gather.5.cloned.1.call-start = ((), (), s32[]{:S(2)}) async-start(), calls=%async_computation.1 | async-start | bytes 3317760 | tf_op jit(solution)/shard_map/all_gather | solution.py:61
  33.2 10.7 %collective-permute-start = (bf16[1,1,32,320]{3,2,1,0:T(8,128)(2,1)S(1)}, bf16[1,1,32,320]{3,2,1,0:T(8,128)(2,1)S(1)}, u32[]{:S(2)}, u32[]{:S(2)}) collective-permute-start(bf16[1,1,32,320]{3,2,1,0:T(8,128)(2,1)S(1)} %get-tuple-element.39), channel_id=1, source_target_pairs={{0,4},{4,8},{8,12},{1,5},{5,9},{9,13},{2,6},{6,10},{10,14},{3,7},{... | collective-permute-start | bytes 61448 | tf_op jit(solution)/shard_map/ppermute | solution.py:17
  36.4 8.4 %collective-permute-start.1 = (bf16[1,1,32,320]{3,2,1,0:T(8,128)(2,1)S(1)}, bf16[1,1,32,320]{3,2,1,0:T(8,128)(2,1)S(1)}, u32[]{:S(2)}, u32[]{:S(2)}) collective-permute-start(bf16[1,1,32,320]{3,2,1,0:T(8,128)(2,1)S(1)} %get-tuple-element.40), channel_id=1, source_target_pairs={{4,0},{8,4},{12,8},{5,1},{9,5},{13,9},{6,2},{10,6},{14,10},{7,3},{... | collective-permute-start | bytes 61448 | tf_op jit(solution)/shard_map/ppermute | solution.py:18
  44.9 9.9 %collective-permute-start.2 = (bf16[1,34,1,320]{3,2,1,0:T(2,128)(2,1)S(1)}, bf16[1,34,1,320]{3,2,1,0:T(2,128)(2,1)S(1)}, u32[]{:S(2)}, u32[]{:S(2)}) collective-permute-start(bf16[1,34,1,320]{3,2,1,0:T(2,128)(2,1)S(1)} %get-tuple-element.32), channel_id=1, source_target_pairs={{0,1},{1,2},{2,3},{4,5},{5,6},{6,7},{8,9},{9,10},{10,11},{12,13},{... | collective-permute-start | bytes 65288 | tf_op jit(solution)/shard_map/ppermute | solution.py:17
  49.7 5.4 %collective-permute-start.3 = (bf16[1,34,1,320]{3,2,1,0:T(2,128)(2,1)S(1)}, bf16[1,34,1,320]{3,2,1,0:T(2,128)(2,1)S(1)}, u32[]{:S(2)}, u32[]{:S(2)}) collective-permute-start(bf16[1,34,1,320]{3,2,1,0:T(2,128)(2,1)S(1)} %get-tuple-element.31), channel_id=1, source_target_pairs={{1,0},{2,1},{3,2},{5,4},{6,5},{7,6},{9,8},{10,9},{11,10},{13,12},{... | collective-permute-start | bytes 65288 | tf_op jit(solution)/shard_map/ppermute | solution.py:18
  78.7 24.7 %copy-start.9 = (f32[320]{0:T(512)S(1)}, f32[320]{0:T(512)}, u32[]{:S(2)}) copy-start(f32[320]{0:T(512)} %param.8) | copy-start | bytes 3844
  104.0 17.0 %collective-permute-start.4 = (bf16[1,1,32,320]{3,2,1,0:T(8,128)(2,1)S(1)}, bf16[1,1,32,320]{3,2,1,0:T(8,128)(2,1)S(1)}, u32[]{:S(2)}, u32[]{:S(2)}) collective-permute-start(bf16[1,1,32,320]{3,2,1,0:T(8,128)(2,1)S(1)} %get-tuple-element.35), channel_id=1, source_target_pairs={{0,4},{4,8},{8,12},{1,5},{5,9},{9,13},{2,6},{6,10},{10,14},{3,7},{... | collective-permute-start | bytes 61448 | tf_op jit(solution)/shard_map/ppermute | solution.py:17
  105.9 15.0 %collective-permute-start.5 = (bf16[1,1,32,320]{3,2,1,0:T(8,128)(2,1)S(1)}, bf16[1,1,32,320]{3,2,1,0:T(8,128)(2,1)S(1)}, u32[]{:S(2)}, u32[]{:S(2)}) collective-permute-start(bf16[1,1,32,320]{3,2,1,0:T(8,128)(2,1)S(1)} %get-tuple-element.36), channel_id=1, source_target_pairs={{4,0},{8,4},{12,8},{5,1},{9,5},{13,9},{6,2},{10,6},{14,10},{7,3},{... | collective-permute-start | bytes 61448 | tf_op jit(solution)/shard_map/ppermute | solution.py:18
  121.1 7.5 %collective-permute-start.6 = (bf16[1,34,1,320]{3,2,1,0:T(2,128)(2,1)S(1)}, bf16[1,34,1,320]{3,2,1,0:T(2,128)(2,1)S(1)}, u32[]{:S(2)}, u32[]{:S(2)}) collective-permute-start(bf16[1,34,1,320]{3,2,1,0:T(2,128)(2,1)S(1)} %get-tuple-element.28), channel_id=1, source_target_pairs={{0,1},{1,2},{2,3},{4,5},{5,6},{6,7},{8,9},{9,10},{10,11},{12,13},{... | collective-permute-start | bytes 65288 | tf_op jit(solution)/shard_map/ppermute | solution.py:17
  123.0 5.6 %collective-permute-start.7 = (bf16[1,34,1,320]{3,2,1,0:T(2,128)(2,1)S(1)}, bf16[1,34,1,320]{3,2,1,0:T(2,128)(2,1)S(1)}, u32[]{:S(2)}, u32[]{:S(2)}) collective-permute-start(bf16[1,34,1,320]{3,2,1,0:T(2,128)(2,1)S(1)} %get-tuple-element.27), channel_id=1, source_target_pairs={{1,0},{2,1},{3,2},{5,4},{6,5},{7,6},{9,8},{10,9},{11,10},{13,12},{... | collective-permute-start | bytes 65288 | tf_op jit(solution)/shard_map/ppermute | solution.py:18
  134.0 2.3 %copy-start.4 = (bf16[1024,320]{0,1:T(8,128)(2,1)S(1)}, bf16[1024,320]{0,1:T(8,128)(2,1)}, u32[]{:S(2)}) copy-start(bf16[1024,320]{0,1:T(8,128)(2,1)} %copy.20) | copy-start | bytes 1966084
  136.3 2.9 %copy-start.5 = (bf16[1024,320]{0,1:T(8,128)(2,1)S(1)}, bf16[1024,320]{0,1:T(8,128)(2,1)}, u32[]{:S(2)}) copy-start(bf16[1024,320]{0,1:T(8,128)(2,1)} %copy.22) | copy-start | bytes 1966084
  136.3 3.8 %copy-start.1 = (f32[1024,320]{0,1:T(8,128)S(1)}, f32[1024,320]{0,1:T(8,128)}, u32[]{:S(2)}) copy-start(f32[1024,320]{0,1:T(8,128)} %get-tuple-element.45) | copy-start | bytes 3932164
  140.0 4.8 %copy-start.2 = (bf16[1,32,32,320]{3,2,1,0:T(8,128)(2,1)S(1)}, bf16[1,32,32,320]{3,2,1,0:T(8,128)(2,1)}, u32[]{:S(2)}) copy-start(bf16[1,32,32,320]{3,2,1,0:T(8,128)(2,1)} %get-tuple-element.13) | copy-start | bytes 1966084
  144.9 2.4 %copy-start.6 = (bf16[1024,320]{0,1:T(8,128)(2,1)S(1)}, bf16[1024,320]{0,1:T(8,128)(2,1)}, u32[]{:S(2)}) copy-start(bf16[1024,320]{0,1:T(8,128)(2,1)} %copy.24) | copy-start | bytes 1966084
  144.9 3.3 %copy-start.3 = (bf16[1024,320]{0,1:T(8,128)(2,1)S(1)}, bf16[1024,320]{0,1:T(8,128)(2,1)}, u32[]{:S(2)}) copy-start(bf16[1024,320]{0,1:T(8,128)(2,1)} %copy.25) | copy-start | bytes 1966084
  147.3 2.7 %copy-start.7 = (bf16[320,9,320]{0,2,1:T(8,128)(2,1)S(1)}, bf16[320,9,320]{0,2,1:T(8,128)(2,1)}, u32[]{:S(2)}) copy-start(bf16[320,9,320]{0,2,1:T(8,128)(2,1)} %copy.27) | copy-start | bytes 5529604
  147.3 2.7 %copy-start.8 = (f32[1024,320]{0,1:T(8,128)S(1)}, f32[1024,320]{0,1:T(8,128)}, u32[]{:S(2)}) copy-start(f32[1024,320]{0,1:T(8,128)} %copy.28) | copy-start | bytes 3932164
Sparse Core Ops, SparseCore 0:
  8.9 35.3 all-gather.2
  45.8 34.6 all-gather.4
where the time goes:
time: 164 us; the launch traced here: 163 us
  local copies, waits for them, and re-layouts  47.5 us (29%)
  blocking collectives  44.6 us (27%)
  starting transfers between devices  35.5 us (22%)
  between operations  13.6 us (8%)
  matrix products  11.6 us (7%)
  other arithmetic  8 us (5%)
  waiting for transfers between devices  2.03 us (1%)
    psum x2, blocking collectives, normalize(): lax.psum((jnp.sum(grouped, axis=(1, 3)), jnp.sum(grouped * grouped, axis=...  44.6 us
    ppermute x4, starting transfers between devices, extended(): after = lax.ppermute(initial, axis, down)  23.6 us
    concatenate x10, local copies, waits for them, and re-layouts, tap_stack(): return jnp.concatenate(pieces, axis=-1).reshape(-1, 9 * width)  20.4 us
    ppermute x4, starting transfers between devices, extended(): before = lax.ppermute(last, axis, up)  11.9 us
    dot_general x2, matrix products, finish(): lax.dot_general(stacked, flat_kernel, (((1,), (1,)), ((), ())), preferred...  11.6 us
    unnamed x27, local copies, waits for them, and re-layouts  9.62 us
    all_gather x2, local copies, waits for them, and re-layouts, convolve_gathered(): whole_kernel = lax.all_gather(kernel, 'dp', axis=0, tiled=True)  8.4 us
    slice x3, local copies, waits for them, and re-layouts, tap_stack(): padded[:, shift_row:shift_row + tile_rows, shift_col:shift_col + tile_col...  3.64 us
  transfers between devices with their start and end apart: 10, of which 2 were waited for; matrix products, arithmetic and copies ran while one was open for 24% of the time, Pallas kernels for 0%

commit v1 on v0

--- a/solution.py
+++ b/solution.py
@@ -58,7 +58,15 @@
 
 
 def convolve_gathered(stacked, kernel, skip_flat):
-    whole_kernel = lax.all_gather(kernel, "dp", axis=0, tiled=True)
+    whole_kernel = jnp.concatenate(
+        lax.all_to_all(
+            jnp.stack(tuple((kernel for _ in range(lax.axis_size("dp"))))),
+            axis_name="dp",
+            split_axis=0,
+            concat_axis=0,
+        ),
+        axis=0,
+    )
     return finish(stacked, whole_kernel, skip_flat)
 
 

time: 164 us -> 183 us (1.12)
  local copies, waits for them, and re-layouts: 47.5 us -> 64.8 us
  between operations: 13.6 us -> 0.28 us
  starting transfers between devices: 35.5 us -> 46 us
  other arithmetic: 8 us -> 13.8 us
  waiting for transfers between devices: 2.03 us -> 0.03 us
    all_to_all x0 -> x2, local copies, waits for them, and re-layouts: none -> 13 us  [convolve_gathered(): lax.all_to_all(jnp.stack(tuple((kernel for _ in range(lax.axis_size('dp')...]
    another operation x0 -> x2, local copies, waits for them, and re-layouts: none -> 10.3 us  [finish(): flat_kernel = whole_kernel.reshape(whole_kernel.shape[0], -1)]
    all_to_all x0 -> x2, starting transfers between devices: none -> 8.7 us  [convolve_gathered(): lax.all_to_all(jnp.stack(tuple((kernel for _ in range(lax.axis_size('dp')...]
    all_gather x2 -> x0, local copies, waits for them, and re-layouts: 8.4 us -> none  [convolve_gathered(): whole_kernel = lax.all_gather(kernel, 'dp', axis=0, tiled=True)]
    another operation x0 -> x2, other arithmetic: none -> 5.22 us  [convolve_gathered(): jnp.stack(tuple((kernel for _ in range(lax.axis_size('dp')))))]
    unnamed x27 -> x29, local copies, waits for them, and re-layouts: 9.62 us -> 9.95 us
  transfers between devices with their start and end apart: 10 -> 10, of which waited for: 2 -> 0; matrix products, arithmetic and copies ran while one was open for 24% -> 32% of each run, Pallas kernels for 0% -> 0%
where the time goes in v1:
time: 183 us; the launch traced here: 181 us
  local copies, waits for them, and re-layouts  64.8 us (35%)
  starting transfers between devices  46 us (25%)
  blocking collectives  44.6 us (24%)
  other arithmetic  13.8 us (8%)
  matrix products  11.6 us (6%)
    psum x2, blocking collectives, normalize(): lax.psum((jnp.sum(grouped, axis=(1, 3)), jnp.sum(grouped * grouped, axis=...  44.6 us
    ppermute x4, starting transfers between devices, extended(): after = lax.ppermute(initial, axis, down)  25 us
    concatenate x10, local copies, waits for them, and re-layouts, tap_stack(): return jnp.concatenate(pieces, axis=-1).reshape(-1, 9 * width)  21.1 us
    all_to_all x2, local copies, waits for them, and re-layouts, convolve_gathered(): lax.all_to_all(jnp.stack(tuple((kernel for _ in range(lax.axis_size('dp')...  13 us
    ppermute x4, starting transfers between devices, extended(): before = lax.ppermute(last, axis, up)  12.3 us
    dot_general x2, matrix products, finish(): lax.dot_general(stacked, flat_kernel, (((1,), (1,)), ((), ())), preferred...  11.6 us
    another operation x2, local copies, waits for them, and re-layouts, finish(): flat_kernel = whole_kernel.reshape(whole_kernel.shape[0], -1)  10.3 us
    unnamed x29, local copies, waits for them, and re-layouts  9.95 us
  transfers between devices with their start and end apart: 10, of which 0 were waited for; matrix products, arithmetic and copies ran while one was open for 32% of the time, Pallas kernels for 0%

profile of v1, /device:TPU:9, one launch (start us, length us, event | category | flops | bytes accessed | tf_op | source)
XLA Modules:
  0.0 181.1 jit_solution(3912073632823896451)
XLA Ops:
  0.0 1.5 convert_reduce_fusion
  1.9 22.3 %all-reduce.1 = (f32[1,32]{1,0:T(1,128)S(1)}, f32[1,32]{1,0:T(1,128)S(1)}) all-reduce(f32[1,32]{1,0:T(1,128)S(1)} %bitcast.67, f32[1,32]{1,0:T(1,128)S(1)} %bitcast.65), channel_id=1, replica_groups=mesh['dp'=2,'row'=4,'col'=4] {'row','col'}, use_global_device_ids=true, to_apply=%region_5.6 | all-reduce | flops 64 | bytes 512 | tf_op jit(solution)/shard_map/psum | solution.py:28
  24.7 1.6 multiply_convert_fusion.1
  26.3 3.2 %collective-permute-start = (bf16[1,1,32,320]{3,2,1,0:T(8,128)(2,1)S(1)}, bf16[1,1,32,320]{3,2,1,0:T(8,128)(2,1)S(1)}, u32[]{:S(2)}, u32[]{:S(2)}) collective-permute-start(bf16[1,1,32,320]{3,2,1,0:T(8,128)(2,1)S(1)} %get-tuple-element.39), channel_id=1, source_target_pairs={{0,4},{4,8},{8,12},{1,5},{5,9},{9,13},{2,6},{6,10},{10,14},{3,7},{... | collective-permute-start | bytes 61448 | tf_op jit(solution)/shard_map/ppermute | solution.py:17
  29.5 7.6 %collective-permute-start.1 = (bf16[1,1,32,320]{3,2,1,0:T(8,128)(2,1)S(1)}, bf16[1,1,32,320]{3,2,1,0:T(8,128)(2,1)S(1)}, u32[]{:S(2)}, u32[]{:S(2)}) collective-permute-start(bf16[1,1,32,320]{3,2,1,0:T(8,128)(2,1)S(1)} %get-tuple-element.40), channel_id=1, source_target_pairs={{4,0},{8,4},{12,8},{5,1},{9,5},{13,9},{6,2},{10,6},{14,10},{7,3},{... | collective-permute-start | bytes 61448 | tf_op jit(solution)/shard_map/ppermute | solution.py:18
  37.1 1.8 %pad_maximum_fusion = bf16[2,160,9,320]{3,1,2,0:T(8,128)(2,1)} fusion(bf16[1,160,9,320]{3,1,2,0:T(8,128)(2,1)S(1)} %bitcast.62), kind=kLoop, calls=%fused_computation | loop fusion | flops 921600 | bytes 2764800 | tf_op jit(solution)/shard_map/stack | solution.py:63
  39.0 3.8 %all-to-all-start = ((bf16[2,160,9,320]{3,1,2,0:T(8,128)(2,1)}), bf16[2,160,9,320]{3,1,2,0:T(8,128)(2,1)S(1)}, u32[]{:S(2)}, u32[]{:S(2)}) async-start(bf16[2,160,9,320]{3,1,2,0:T(8,128)(2,1)} %pad_maximum_fusion), calls=%async_computation | async-start | bytes 4423680 | tf_op jit(solution)/shard_map/all_to_all | solution.py:62
  42.8 3.4 %pad_maximum_fusion.1 = bf16[2,160,9,320]{3,1,2,0:T(8,128)(2,1)} fusion(bf16[1,160,9,320]{3,1,2,0:T(8,128)(2,1)} %bitcast.63), kind=kLoop, calls=%fused_computation.1 | loop fusion | flops 921600 | bytes 2764800 | tf_op jit(solution)/shard_map/stack | solution.py:63
  46.3 3.3 %collective-permute-start.2 = (bf16[1,34,1,320]{3,2,1,0:T(2,128)(2,1)S(1)}, bf16[1,34,1,320]{3,2,1,0:T(2,128)(2,1)S(1)}, u32[]{:S(2)}, u32[]{:S(2)}) collective-permute-start(bf16[1,34,1,320]{3,2,1,0:T(2,128)(2,1)S(1)} %get-tuple-element.32), channel_id=1, source_target_pairs={{0,1},{1,2},{2,3},{4,5},{5,6},{6,7},{8,9},{9,10},{10,11},{12,13},{... | collective-permute-start | bytes 65288 | tf_op jit(solution)/shard_map/ppermute | solution.py:17
  49.5 4.6 %collective-permute-start.3 = (bf16[1,34,1,320]{3,2,1,0:T(2,128)(2,1)S(1)}, bf16[1,34,1,320]{3,2,1,0:T(2,128)(2,1)S(1)}, u32[]{:S(2)}, u32[]{:S(2)}) collective-permute-start(bf16[1,34,1,320]{3,2,1,0:T(2,128)(2,1)S(1)} %get-tuple-element.31), channel_id=1, source_target_pairs={{1,0},{2,1},{3,2},{5,4},{6,5},{7,6},{9,8},{10,9},{11,10},{13,12},{... | collective-permute-start | bytes 65288 | tf_op jit(solution)/shard_map/ppermute | solution.py:18
  54.2 1.4 pad_maximum_fusion.6
  56.2 2.6 %fusion.6 = (bf16[1,32,32,320]{3,2,1,0:T(8,128)(2,1)}, bf16[1,32,32,320]{3,2,1,0:T(8,128)(2,1)}, bf16[1,32,32,320]{3,2,1,0:T(8,128)(2,1)}, bf16[1,32,32,320]{3,2...) fusion(bf16[1,34,33,320]{3,2,1,0:T(8,128)(2,1)S(1)} %get-tuple-element.29, ...), kind=kLoop, calls=%fused_computation.42 | loop fusion | bytes 7864320 | tf_op jit(solution)/shard_map/slice | solution.py:43
  58.7 10.4 %concatenate.96 = bf16[1024,2880]{1,0:T(8,128)(2,1)} concatenate(bf16[1024,320]{1,0:T(8,128)(2,1)} %bitcast.49, bf16[1024,320]{1,0:T(8,128)(2,1)} %bitcast.54, bf16[1024,320]{1,0:T(8,128)(2,1)} %bitcast.48, bf16[1024,320]{1,0:T(8,128)(2,1)} %bitcast.50, bf16[1024,320]{1,0:T(8,128)(2,1)S(1)} %bitcast.43, bf16[1024,320]{1,0:T(8,128)(2,1)} %bitcast.47, bf16[1024,320]{1,0:T(8,128)(2,1)} %bitcast.51, ...), dimensions={1} | concatenate | bytes 11796480 | tf_op jit(solution)/shard_map/concatenate | solution.py:47
  69.2 1.4 copy-done
  70.5 4.9 %all-to-all-start.1 = ((bf16[2,160,9,320]{3,1,2,0:T(8,128)(2,1)}), bf16[2,160,9,320]{3,1,2,0:T(8,128)(2,1)}, u32[]{:S(2)}, u32[]{:S(2)}) async-start(bf16[2,160,9,320]{3,1,2,0:T(8,128)(2,1)} %pad_maximum_fusion.1), calls=%async_computation.1 | async-start | bytes 4423680 | tf_op jit(solution)/shard_map/all_to_all | solution.py:62
  75.4 5.9 %copy.17 = bf16[2,160,9,320]{1,0,3,2:T(2,128)(2,1)S(1)} copy(bf16[2,160,9,320]{3,1,2,0:T(8,128)(2,1)} %copy-done) | data formatting | bytes 3686400 | tf_op jit(solution)/shard_map/all_to_all | solution.py:62
  81.4 2.9 %reshape_reshape.6 = bf16[320,2880]{0,1:T(8,128)(2,1)} reshape(bf16[2,160,9,320]{1,0,3,2:T(2,128)(2,1)S(1)} %copy.17) | data formatting | bytes 3686400 | tf_op jit(solution)/shard_map/reshape;reshape | solution.py:51
  84.2 6.7 %fusion.3 = (f32[320]{0:T(512)S(1)}, f32[320]{0:T(512)S(1)}, f32[1024,320]{0,1:T(8,128)}) fusion(bf16[1024,2880]{1,0:T(8,128)(2,1)} %concatenate.96, bf16[320,2880]{0,1:T(8,128)(2,1)} %reshape_reshape.6), kind=kOutput, calls=%fused_computation.39 | convolution fusion | flops 1889074688 | bytes 9054720 | tf_op jit(solution)/shard_map/dot_general | solution.py:52
  91.4 22.3 %all-reduce = (f32[1,32]{1,0:T(1,128)S(1)}, f32[1,32]{1,0:T(1,128)S(1)}) all-reduce(f32[1,32]{1,0:T(1,128)S(1)} %bitcast.66, f32[1,32]{1,0:T(1,128)S(1)} %bitcast.64), channel_id=1, replica_groups=mesh['dp'=2,'row'=4,'col'=4] {'row','col'}, use_global_device_ids=true, to_apply=%region_11.12 | all-reduce | flops 64 | bytes 512 | tf_op jit(solution)/shard_map/psum | solution.py:28
  114.1 1.9 %copy.18 = f32[1024,320]{1,0:T(8,128)S(1)} copy(f32[1024,320]{0,1:T(8,128)} %get-tuple-element.45) | data formatting | bytes 2621440 | tf_op jit(solution)/shard_map/convert_element_type | solution.py:25
  116.5 1.9 %collective-permute-start.4 = (bf16[1,1,32,320]{3,2,1,0:T(8,128)(2,1)S(1)}, bf16[1,1,32,320]{3,2,1,0:T(8,128)(2,1)S(1)}, u32[]{:S(2)}, u32[]{:S(2)}) collective-permute-start(bf16[1,1,32,320]{3,2,1,0:T(8,128)(2,1)S(1)} %get-tuple-element.35), channel_id=1, source_target_pairs={{0,4},{4,8},{8,12},{1,5},{5,9},{9,13},{2,6},{6,10},{10,14},{3,7},{... | collective-permute-start | bytes 61448 | tf_op jit(solution)/shard_map/ppermute | solution.py:17
  118.4 8.0 %collective-permute-start.5 = (bf16[1,1,32,320]{3,2,1,0:T(8,128)(2,1)S(1)}, bf16[1,1,32,320]{3,2,1,0:T(8,128)(2,1)S(1)}, u32[]{:S(2)}, u32[]{:S(2)}) collective-permute-start(bf16[1,1,32,320]{3,2,1,0:T(8,128)(2,1)S(1)} %get-tuple-element.36), channel_id=1, source_target_pairs={{4,0},{8,4},{12,8},{5,1},{9,5},{13,9},{6,2},{10,6},{14,10},{7,3},{... | collective-permute-start | bytes 61448 | tf_op jit(solution)/shard_map/ppermute | solution.py:18
  127.8 7.1 %copy.27 = bf16[2,160,9,320]{1,0,3,2:T(2,128)(2,1)} copy(bf16[2,160,9,320]{3,1,2,0:T(8,128)(2,1)} %all-to-all-done.1) | data formatting | bytes 3686400 | tf_op jit(solution)/shard_map/all_to_all | solution.py:62
  134.9 7.4 %reshape_reshape.7 = bf16[320,2880]{0,1:T(8,128)(2,1)} reshape(bf16[2,160,9,320]{1,0,3,2:T(2,128)(2,1)} %copy.27) | data formatting | bytes 3686400 | tf_op jit(solution)/shard_map/reshape;reshape | solution.py:51
  142.4 3.9 %collective-permute-start.6 = (bf16[1,34,1,320]{3,2,1,0:T(2,128)(2,1)S(1)}, bf16[1,34,1,320]{3,2,1,0:T(2,128)(2,1)S(1)}, u32[]{:S(2)}, u32[]{:S(2)}) collective-permute-start(bf16[1,34,1,320]{3,2,1,0:T(2,128)(2,1)S(1)} %get-tuple-element.28), channel_id=1, source_target_pairs={{0,1},{1,2},{2,3},{4,5},{5,6},{6,7},{8,9},{9,10},{10,11},{12,13},{... | collective-permute-start | bytes 65288 | tf_op jit(solution)/shard_map/ppermute | solution.py:17
  146.3 4.8 %collective-permute-start.7 = (bf16[1,34,1,320]{3,2,1,0:T(2,128)(2,1)S(1)}, bf16[1,34,1,320]{3,2,1,0:T(2,128)(2,1)S(1)}, u32[]{:S(2)}, u32[]{:S(2)}) collective-permute-start(bf16[1,34,1,320]{3,2,1,0:T(2,128)(2,1)S(1)} %get-tuple-element.27), channel_id=1, source_target_pairs={{1,0},{2,1},{3,2},{5,4},{6,5},{7,6},{9,8},{10,9},{11,10},{13,12},{... | collective-permute-start | bytes 65288 | tf_op jit(solution)/shard_map/ppermute | solution.py:18
  157.9 2.3 %copy.21 = bf16[1024,320]{0,1:T(8,128)(2,1)} copy(bf16[1024,320]{1,0:T(8,128)(2,1)} %bitcast.59) | data formatting | bytes 1310720 | tf_op jit(solution)/shard_map/concatenate | solution.py:47
  160.2 2.2 %copy.22 = bf16[1024,320]{0,1:T(8,128)(2,1)} copy(bf16[1024,320]{1,0:T(8,128)(2,1)} %bitcast.57) | data formatting | bytes 1310720 | tf_op jit(solution)/shard_map/concatenate | solution.py:47
  163.3 2.0 %constant_dynamic-update-slice_fusion.5 = bf16[1024,2880]{0,1:T(8,128)(2,1)} fusion(bf16[1024,2880]{0,1:T(8,128)(2,1)} %constant_dynamic-update-slice_fusion.6, bf16[1024,320]{0,1:T(8,128)(2,1)} %copy.21), kind=kLoop, calls=%fused_computation.32 | loop fusion | bytes 1310720
  166.2 1.4 fusion.2
  171.1 2.1 %constant_dynamic-update-slice_fusion.2 = bf16[1024,2880]{0,1:T(8,128)(2,1)} fusion(bf16[1024,2880]{0,1:T(8,128)(2,1)} %constant_dynamic-update-slice_fusion.3, bf16[1024,320]{0,1:T(8,128)(2,1)} %copy.24), kind=kLoop, calls=%fused_computation.29 | loop fusion | bytes 1310720
  175.0 4.9 %fusion = bf16[1024,320]{0,1:T(8,128)(2,1)S(1)} fusion(f32[1024,320]{0,1:T(8,128)S(1)} %copy-done.8, bf16[1024,2880]{0,1:T(8,128)(2,1)} %constant_dynamic-update-slice_fusion, bf16[320,2880]{0,1:T(8,128)(2,1)S(1)} %copy-done.7), kind=kOutput, calls=%fused_computation.6 | convolution fusion | flops 1888092160 | bytes 9707520 | tf_op jit(solution)/shard_map/dot_general | solution.py:52
  (73 shorter events, 19.3 us)
Async XLA Ops:
  0.0 37.1 %copy-start.9 = (bf16[160,9,320]{2,0,1:T(8,128)(2,1)S(1)}, bf16[160,9,320]{2,0,1:T(8,128)(2,1)}, u32[]{:S(2)}) copy-start(bf16[160,9,320]{2,0,1:T(8,128)(2,1)} %param.7) | copy-start | bytes 2764804
  26.3 19.8 %collective-permute-start = (bf16[1,1,32,320]{3,2,1,0:T(8,128)(2,1)S(1)}, bf16[1,1,32,320]{3,2,1,0:T(8,128)(2,1)S(1)}, u32[]{:S(2)}, u32[]{:S(2)}) collective-permute-start(bf16[1,1,32,320]{3,2,1,0:T(8,128)(2,1)S(1)} %get-tuple-element.39), channel_id=1, source_target_pairs={{0,4},{4,8},{8,12},{1,5},{5,9},{9,13},{2,6},{6,10},{10,14},{3,7},{... | collective-permute-start | bytes 61448 | tf_op jit(solution)/shard_map/ppermute | solution.py:17
  29.5 16.6 %collective-permute-start.1 = (bf16[1,1,32,320]{3,2,1,0:T(8,128)(2,1)S(1)}, bf16[1,1,32,320]{3,2,1,0:T(8,128)(2,1)S(1)}, u32[]{:S(2)}, u32[]{:S(2)}) collective-permute-start(bf16[1,1,32,320]{3,2,1,0:T(8,128)(2,1)S(1)} %get-tuple-element.40), channel_id=1, source_target_pairs={{4,0},{8,4},{12,8},{5,1},{9,5},{13,9},{6,2},{10,6},{14,10},{7,3},{... | collective-permute-start | bytes 61448 | tf_op jit(solution)/shard_map/ppermute | solution.py:18
  39.0 30.2 %all-to-all-start = ((bf16[2,160,9,320]{3,1,2,0:T(8,128)(2,1)}), bf16[2,160,9,320]{3,1,2,0:T(8,128)(2,1)S(1)}, u32[]{:S(2)}, u32[]{:S(2)}) async-start(bf16[2,160,9,320]{3,1,2,0:T(8,128)(2,1)} %pad_maximum_fusion), calls=%async_computation | async-start | bytes 4423680 | tf_op jit(solution)/shard_map/all_to_all | solution.py:62
  46.3 9.3 %collective-permute-start.2 = (bf16[1,34,1,320]{3,2,1,0:T(2,128)(2,1)S(1)}, bf16[1,34,1,320]{3,2,1,0:T(2,128)(2,1)S(1)}, u32[]{:S(2)}, u32[]{:S(2)}) collective-permute-start(bf16[1,34,1,320]{3,2,1,0:T(2,128)(2,1)S(1)} %get-tuple-element.32), channel_id=1, source_target_pairs={{0,1},{1,2},{2,3},{4,5},{5,6},{6,7},{8,9},{9,10},{10,11},{12,13},{... | collective-permute-start | bytes 65288 | tf_op jit(solution)/shard_map/ppermute | solution.py:17
  49.5 6.0 %collective-permute-start.3 = (bf16[1,34,1,320]{3,2,1,0:T(2,128)(2,1)S(1)}, bf16[1,34,1,320]{3,2,1,0:T(2,128)(2,1)S(1)}, u32[]{:S(2)}, u32[]{:S(2)}) collective-permute-start(bf16[1,34,1,320]{3,2,1,0:T(2,128)(2,1)S(1)} %get-tuple-element.31), channel_id=1, source_target_pairs={{1,0},{2,1},{3,2},{5,4},{6,5},{7,6},{9,8},{10,9},{11,10},{13,12},{... | collective-permute-start | bytes 65288 | tf_op jit(solution)/shard_map/ppermute | solution.py:18
  69.2 1.4 copy-start
  70.5 57.3 %all-to-all-start.1 = ((bf16[2,160,9,320]{3,1,2,0:T(8,128)(2,1)}), bf16[2,160,9,320]{3,1,2,0:T(8,128)(2,1)}, u32[]{:S(2)}, u32[]{:S(2)}) async-start(bf16[2,160,9,320]{3,1,2,0:T(8,128)(2,1)} %pad_maximum_fusion.1), calls=%async_computation.1 | async-start | bytes 4423680 | tf_op jit(solution)/shard_map/all_to_all | solution.py:62
  91.0 25.0 %copy-start.10 = (f32[320]{0:T(512)S(1)}, f32[320]{0:T(512)}, u32[]{:S(2)}) copy-start(f32[320]{0:T(512)} %param.8) | copy-start | bytes 3844
  114.1 12.4 %copy-start.1 = (bf16[1,32,32,320]{3,2,1,0:T(8,128)(2,1)S(1)}, bf16[1,32,32,320]{3,2,1,0:T(8,128)(2,1)}, u32[]{:S(2)}) copy-start(bf16[1,32,32,320]{3,2,1,0:T(8,128)(2,1)} %param.5) | copy-start | bytes 1966084
  116.5 25.8 %collective-permute-start.4 = (bf16[1,1,32,320]{3,2,1,0:T(8,128)(2,1)S(1)}, bf16[1,1,32,320]{3,2,1,0:T(8,128)(2,1)S(1)}, u32[]{:S(2)}, u32[]{:S(2)}) collective-permute-start(bf16[1,1,32,320]{3,2,1,0:T(8,128)(2,1)S(1)} %get-tuple-element.35), channel_id=1, source_target_pairs={{0,4},{4,8},{8,12},{1,5},{5,9},{9,13},{2,6},{6,10},{10,14},{3,7},{... | collective-permute-start | bytes 61448 | tf_op jit(solution)/shard_map/ppermute | solution.py:17
  118.4 23.9 %collective-permute-start.5 = (bf16[1,1,32,320]{3,2,1,0:T(8,128)(2,1)S(1)}, bf16[1,1,32,320]{3,2,1,0:T(8,128)(2,1)S(1)}, u32[]{:S(2)}, u32[]{:S(2)}) collective-permute-start(bf16[1,1,32,320]{3,2,1,0:T(8,128)(2,1)S(1)} %get-tuple-element.36), channel_id=1, source_target_pairs={{4,0},{8,4},{12,8},{5,1},{9,5},{13,9},{6,2},{10,6},{14,10},{7,3},{... | collective-permute-start | bytes 61448 | tf_op jit(solution)/shard_map/ppermute | solution.py:18
  142.4 11.3 %collective-permute-start.6 = (bf16[1,34,1,320]{3,2,1,0:T(2,128)(2,1)S(1)}, bf16[1,34,1,320]{3,2,1,0:T(2,128)(2,1)S(1)}, u32[]{:S(2)}, u32[]{:S(2)}) collective-permute-start(bf16[1,34,1,320]{3,2,1,0:T(2,128)(2,1)S(1)} %get-tuple-element.28), channel_id=1, source_target_pairs={{0,1},{1,2},{2,3},{4,5},{5,6},{6,7},{8,9},{9,10},{10,11},{12,13},{... | collective-permute-start | bytes 65288 | tf_op jit(solution)/shard_map/ppermute | solution.py:17
  146.3 7.4 %collective-permute-start.7 = (bf16[1,34,1,320]{3,2,1,0:T(2,128)(2,1)S(1)}, bf16[1,34,1,320]{3,2,1,0:T(2,128)(2,1)S(1)}, u32[]{:S(2)}, u32[]{:S(2)}) collective-permute-start(bf16[1,34,1,320]{3,2,1,0:T(2,128)(2,1)S(1)} %get-tuple-element.27), channel_id=1, source_target_pairs={{1,0},{2,1},{3,2},{5,4},{6,5},{7,6},{9,8},{10,9},{11,10},{13,12},{... | collective-permute-start | bytes 65288 | tf_op jit(solution)/shard_map/ppermute | solution.py:18
  157.9 4.5 %copy-start.4 = (bf16[1024,320]{0,1:T(8,128)(2,1)S(1)}, bf16[1024,320]{0,1:T(8,128)(2,1)}, u32[]{:S(2)}) copy-start(bf16[1024,320]{0,1:T(8,128)(2,1)} %copy.20) | copy-start | bytes 1966084
  162.4 2.9 %copy-start.6 = (bf16[1024,320]{0,1:T(8,128)(2,1)S(1)}, bf16[1024,320]{0,1:T(8,128)(2,1)}, u32[]{:S(2)}) copy-start(bf16[1024,320]{0,1:T(8,128)(2,1)} %copy.22) | copy-start | bytes 1966084
  162.4 3.8 %copy-start.2 = (f32[1024,320]{0,1:T(8,128)S(1)}, f32[1024,320]{0,1:T(8,128)}, u32[]{:S(2)}) copy-start(f32[1024,320]{0,1:T(8,128)} %get-tuple-element.45) | copy-start | bytes 3932164
  168.7 1.5 copy-start.5
  169.9 3.3 %copy-start.3 = (bf16[1024,320]{0,1:T(8,128)(2,1)S(1)}, bf16[1024,320]{0,1:T(8,128)(2,1)}, u32[]{:S(2)}) copy-start(bf16[1024,320]{0,1:T(8,128)(2,1)} %copy.25) | copy-start | bytes 1966084
  171.1 3.9 %copy-start.7 = (bf16[320,2880]{0,1:T(8,128)(2,1)S(1)}, bf16[320,2880]{0,1:T(8,128)(2,1)}, u32[]{:S(2)}) copy-start(bf16[320,2880]{0,1:T(8,128)(2,1)} %reshape_reshape.7) | copy-start | bytes 5529604
  171.1 3.9 %copy-start.8 = (f32[1024,320]{0,1:T(8,128)S(1)}, f32[1024,320]{0,1:T(8,128)}, u32[]{:S(2)}) copy-start(f32[1024,320]{0,1:T(8,128)} %copy.28) | copy-start | bytes 3932164
